TPU v7x, 128 devices: a whole 4x4x4 slice. The times are simulated.
128 devices in a mesh: sx: 16 (over z, y), sy: 8 (over x, core).
Axes of the slice: x: 4, y: 4, z: 4, core: 2. Of those that a mesh axis runs over, the one named last changes fastest.
Arguments:
- obs_values: bfloat16 [32768, 64], P(('sx', 'sy')), may hold values from -6 to 6
- obs_dest: int32 [32768, 1], P(('sx', 'sy')), may hold values from 0 to 127; in each aligned block of 256 rows (0 to 255, 256 to 511, ...) at most 4 rows name the same one
- obs_node: int32 [32768], P(('sx', 'sy')), may hold values from 0 to 2047
- schur: bfloat16 [16, 8, 2048, 2048], P('sx', 'sy'), as said below
- local_inverse: bfloat16 [16, 8, 2048, 2048], P('sx', 'sy'), as said below
- coarse_inverse: float32 [1024, 1024], P(('sx', 'sy')), as said below
Outputs:
- solution_field: float32 [16, 8, 64, 2048], P('sx', 'sy')
- residual: float32 [16, 8, 64, 2048], P('sx', 'sy')
Inputs may be any that keep to these rules, and one draw needn't show every extreme that they name: `obs_dest`: at most 4 observations of one device go to one subdomain. `schur`: symmetric positive definite. `local_inverse`: symmetric positive definite. `coarse_inverse`: symmetric positive definite.
All inputs are finite; a program needn't handle non-finite values.
Results may differ from a plain program's by a relative error of at most 0.04.
Values may be sent and summed in bfloat16 or wider, within the bound.
A program may use at most 128 MiB of HBM per device.

v0:
```python
import jax
import jax.numpy as jnp
from jax import lax
from jax.sharding import PartitionSpec as P

ITERS = 6


def shortened(array):

    def short(part):
        return part.astype(jnp.bfloat16) if part.dtype == jnp.float32 else part

    return jax.tree.map(short, array)


def padded_2(cells, sides, width):
    for axis, dim in sides:
        count = lax.axis_size(axis)
        ends = count - 1
        head = lax.slice_in_dim(cells, 0, width, axis=dim)
        tail = lax.slice_in_dim(cells, cells.shape[dim] - width, cells.shape[dim], axis=dim)
        cells = jnp.concatenate(
            [
                lax.ppermute(tail, axis, [(i, (i + 1) % count) for i in range(ends)]),
                cells,
                lax.ppermute(head, axis, [((i + 1) % count, i) for i in range(ends)]),
            ],
            axis=dim,
        )
    return cells


def edge_weights(size):
    edge_len = size // 4
    col_index = lax.axis_index("sx")
    row_index = lax.axis_index("sy")
    col_count = lax.axis_size("sx")
    row_count = lax.axis_size("sy")
    sides = (
        jnp.where(col_index > 0, 0.5, 1.0),
        jnp.where(col_index < col_count - 1, 0.5, 1.0),
        jnp.where(row_index > 0, 0.5, 1.0),
        jnp.where(row_index < row_count - 1, 0.5, 1.0),
    )
    return jnp.concatenate([jnp.full((edge_len,), value, jnp.float32) for value in sides])


def coarse_basis(size, count):
    edge_len = size // 4
    node = jnp.arange(size)
    side = node // edge_len
    offset = (node % edge_len).astype(jnp.float32) - (edge_len - 1) / 2.0
    norm_ramp = jnp.sqrt(jnp.float32(edge_len * (edge_len * edge_len - 1) / 12.0))
    column = jnp.arange(count)
    on_edge = side[:, None] == (column // 2)[None, :]
    value = jnp.where(
        (column % 2 == 0)[None, :],
        1.0 / jnp.sqrt(jnp.float32(edge_len)),
        offset[:, None] / norm_ramp,
    )
    return jnp.where(on_edge, value, 0.0)


def assemble(local):
    edge_len = local.shape[1] // 4
    west_part = local[:, 0:edge_len]
    east_part = local[:, edge_len : 2 * edge_len]
    south_part = local[:, 2 * edge_len : 3 * edge_len]
    north_part = local[:, 3 * edge_len :]
    padded = padded_2(shortened(local[None, None]), (("sx", 0), ("sy", 1)), 1)
    west = west_part + padded[0, 1, :, edge_len : 2 * edge_len]
    east = east_part + padded[2, 1, :, 0:edge_len]
    south = south_part + padded[1, 0, :, 3 * edge_len :]
    north = north_part + padded[1, 2, :, 2 * edge_len : 3 * edge_len]
    return jnp.concatenate([west, east, south, north], axis=1)


def gather_coarse(coarse_local):
    return lax.all_gather(coarse_local, ("sx", "sy"), axis=0, tiled=True)


def body(obs_values, obs_dest, obs_node, schur, local_inverse, coarse_inverse):
    hp = lax.Precision.HIGHEST
    size = schur.shape[-1]
    count = coarse_inverse.shape[0]
    realiz = obs_values.shape[1]
    obs_count = obs_values.shape[0]
    row_count = lax.axis_size("sy")
    dev_count = lax.axis_size("sx") * row_count
    target = obs_dest[:, 0]
    capacity = max(2, 2 * obs_count // dev_count)
    match_table = (target[:, None] == jnp.arange(dev_count)[None, :]).astype(jnp.int32)
    slot_index = jnp.sum(jnp.cumsum(match_table, axis=0) * match_table, axis=1) - 1
    position = target * capacity + slot_index
    send_values = (
        jnp.zeros((dev_count * capacity, realiz), jnp.bfloat16).at[position].set(obs_values)
    )
    send_nodes = jnp.zeros((dev_count * capacity,), jnp.int32).at[position].set(obs_node)
    got_values, got_nodes = (
        lax.all_to_all(
            send_values.reshape(dev_count, capacity, realiz),
            ("sx", "sy"),
            split_axis=0,
            concat_axis=0,
            tiled=True,
        ),
        lax.all_to_all(
            send_nodes.reshape(dev_count, capacity),
            ("sx", "sy"),
            split_axis=0,
            concat_axis=0,
            tiled=True,
        ),
    )
    load = jax.ops.segment_sum(
        got_values.reshape(-1, realiz).astype(jnp.float32), got_nodes.reshape(-1), num_segments=size
    )
    rhs = assemble(load.T)
    weight = edge_weights(size)[None, :]
    basis = coarse_basis(size, count)
    schur_mat = schur[0, 0]
    inverse_mat = local_inverse[0, 0]

    def project(vec):
        return jnp.dot(weight * vec, basis, precision=hp).T

    def precond(vec, coarse_all):
        scaled = weight * vec
        part = jnp.dot(scaled.astype(jnp.bfloat16), inverse_mat, preferred_element_type=jnp.float32)
        solved = jnp.dot(coarse_inverse, coarse_all, precision=hp)
        correction = jnp.dot(solved.T, basis.T, precision=hp)
        return assemble(weight * (part + correction))

    def products(left, right):
        return lax.psum(jnp.sum(weight * left * right, axis=1), ("sx", "sy"))

    solution_field = jnp.zeros_like(rhs)
    residual = rhs
    coarse_resid = gather_coarse(project(residual))
    precon = precond(residual, coarse_resid)
    direction = precon
    rz_now = products(residual, precon)
    for step in range(ITERS):
        image = assemble(
            jnp.dot(direction.astype(jnp.bfloat16), schur_mat, preferred_element_type=jnp.float32)
        )
        curv_local = jnp.sum(weight * direction * image, axis=1)
        curv = lax.psum(curv_local, ("sx", "sy"))
        alpha = rz_now / curv
        solution_field = solution_field + alpha[:, None] * direction
        residual = residual - alpha[:, None] * image
        if step < ITERS - 1:
            coarse_resid = gather_coarse(project(residual))
            precon = precond(residual, coarse_resid)
            rz_next = products(residual, precon)
            direction = precon + (rz_next / rz_now)[:, None] * direction
            rz_now = rz_next
    return (solution_field[None, None], residual[None, None])


def solution(mesh):
    placed = (
        P(("sx", "sy"), None),
        P(("sx", "sy"), None),
        P(("sx", "sy")),
        P("sx", "sy", None, None),
        P("sx", "sy", None, None),
        P(("sx", "sy"), None),
    )
    return jax.shard_map(
        body,
        mesh=mesh,
        in_specs=placed,
        out_specs=(P("sx", "sy", None, None), P("sx", "sy", None, None)),
        check_vma=False,
    )
```

profile of v0, /device:TPU:1, one launch (start us, length us, event | category | flops | bytes accessed | tf_op | source)
XLA Modules:
  0.0 1431.5 jit_solution(6117860953516433841)
XLA Ops:
  5.6 11.5 all-to-all-start
  32.6 8.1 all-to-all-done.1
  61.4 7.6 collective-permute-done.3
  73.4 38.2 %all_gather.18 = f32[1024,64]{1,0:T(8,128)S(1)} all-gather(f32[8,64]{1,0:T(8,128)S(1)} %fusion.35), channel_id=1, replica_groups=mesh['sx'=16,'sy'=8] {'sx','sy'}, dimensions={0}, use_global_device_ids=true | all-gather | bytes 264192 | tf_op jit(solution)/shard_map/all_gather | solution.py:80
  134.9 7.7 collective-permute-done.7
  162.2 7.7 collective-permute-done.11
  171.5 70.1 %all-reduce = (f32[64]{0:T(128)S(1)}, f32[64]{0:T(128)S(1)}) all-reduce(f32[64]{0:T(128)S(1)} %get-tuple-element.3, f32[64]{0:T(128)S(1)} %get-tuple-element.2), channel_id=1, replica_groups=mesh['sx'=16,'sy'=8] {'sx','sy'}, use_global_device_ids=true, to_apply=%region_7.8 | all-reduce | flops 128 | bytes 1024 | tf_op jit(solution)/shard_map/psum | solution.py:136
  249.0 34.6 %all_gather.19 = f32[1024,64]{1,0:T(8,128)S(1)} all-gather(f32[8,64]{1,0:T(8,128)S(1)} %fusion.34), channel_id=1, replica_groups=mesh['sx'=16,'sy'=8] {'sx','sy'}, dimensions={0}, use_global_device_ids=true | all-gather | bytes 264192 | tf_op jit(solution)/shard_map/all_gather | solution.py:80
  301.8 7.7 collective-permute-done.15
  311.0 67.8 %psum.86 = f32[64]{0:T(128)S(1)} all-reduce(f32[64]{0:T(128)S(1)} %multiply_reduce_fusion.8), channel_id=1, replica_groups=mesh['sx'=16,'sy'=8] {'sx','sy'}, use_global_device_ids=true, to_apply=%region_11.12 | all-reduce | flops 64 | bytes 512 | tf_op jit(solution)/shard_map/psum | solution.py:136
  399.7 7.3 collective-permute-done.19
  408.9 68.1 %psum.87 = f32[64]{0:T(128)S(1)} all-reduce(f32[64]{0:T(128)S(1)} %multiply_reduce_fusion.7), channel_id=1, replica_groups=mesh['sx'=16,'sy'=8] {'sx','sy'}, use_global_device_ids=true, to_apply=%region_13.14 | all-reduce | flops 64 | bytes 512 | tf_op jit(solution)/shard_map/psum | solution.py:149
  484.4 34.8 %all_gather.20 = f32[1024,64]{1,0:T(8,128)S(1)} all-gather(f32[8,64]{1,0:T(8,128)S(1)} %fusion.33), channel_id=1, replica_groups=mesh['sx'=16,'sy'=8] {'sx','sy'}, dimensions={0}, use_global_device_ids=true | all-gather | bytes 264192 | tf_op jit(solution)/shard_map/all_gather | solution.py:80
  537.4 7.7 collective-permute-done.23
  547.3 68.0 %psum.88 = f32[64]{0:T(128)S(1)} all-reduce(f32[64]{0:T(128)S(1)} %multiply_reduce_fusion.6), channel_id=1, replica_groups=mesh['sx'=16,'sy'=8] {'sx','sy'}, use_global_device_ids=true, to_apply=%region_15.16 | all-reduce | flops 64 | bytes 512 | tf_op jit(solution)/shard_map/psum | solution.py:136
  637.3 7.3 collective-permute-done.27
  646.4 68.1 %psum.89 = f32[64]{0:T(128)S(1)} all-reduce(f32[64]{0:T(128)S(1)} %multiply_reduce_fusion.5), channel_id=1, replica_groups=mesh['sx'=16,'sy'=8] {'sx','sy'}, use_global_device_ids=true, to_apply=%region_17.18 | all-reduce | flops 64 | bytes 512 | tf_op jit(solution)/shard_map/psum | solution.py:149
  723.1 34.5 %all_gather.21 = f32[1024,64]{1,0:T(8,128)S(1)} all-gather(f32[8,64]{1,0:T(8,128)S(1)} %fusion.32), channel_id=1, replica_groups=mesh['sx'=16,'sy'=8] {'sx','sy'}, dimensions={0}, use_global_device_ids=true | all-gather | bytes 264192 | tf_op jit(solution)/shard_map/all_gather | solution.py:80
  775.8 7.7 collective-permute-done.31
  785.0 68.0 %psum.90 = f32[64]{0:T(128)S(1)} all-reduce(f32[64]{0:T(128)S(1)} %multiply_reduce_fusion.4), channel_id=1, replica_groups=mesh['sx'=16,'sy'=8] {'sx','sy'}, use_global_device_ids=true, to_apply=%region_19.20 | all-reduce | flops 64 | bytes 512 | tf_op jit(solution)/shard_map/psum | solution.py:136
  873.9 7.3 collective-permute-done.35
  883.1 68.1 %psum.91 = f32[64]{0:T(128)S(1)} all-reduce(f32[64]{0:T(128)S(1)} %multiply_reduce_fusion.3), channel_id=1, replica_groups=mesh['sx'=16,'sy'=8] {'sx','sy'}, use_global_device_ids=true, to_apply=%region_21.22 | all-reduce | flops 64 | bytes 512 | tf_op jit(solution)/shard_map/psum | solution.py:149
  958.6 34.6 %all_gather.22 = f32[1024,64]{1,0:T(8,128)S(1)} all-gather(f32[8,64]{1,0:T(8,128)S(1)} %fusion.31), channel_id=1, replica_groups=mesh['sx'=16,'sy'=8] {'sx','sy'}, dimensions={0}, use_global_device_ids=true | all-gather | bytes 264192 | tf_op jit(solution)/shard_map/all_gather | solution.py:80
  1011.4 7.7 collective-permute-done.39
  1021.4 68.0 %psum.92 = f32[64]{0:T(128)S(1)} all-reduce(f32[64]{0:T(128)S(1)} %multiply_reduce_fusion.2), channel_id=1, replica_groups=mesh['sx'=16,'sy'=8] {'sx','sy'}, use_global_device_ids=true, to_apply=%region_23.24 | all-reduce | flops 64 | bytes 512 | tf_op jit(solution)/shard_map/psum | solution.py:136
  1111.3 7.3 collective-permute-done.43
  1120.5 68.1 %psum.93 = f32[64]{0:T(128)S(1)} all-reduce(f32[64]{0:T(128)S(1)} %multiply_reduce_fusion.1), channel_id=1, replica_groups=mesh['sx'=16,'sy'=8] {'sx','sy'}, use_global_device_ids=true, to_apply=%region_25.26 | all-reduce | flops 64 | bytes 512 | tf_op jit(solution)/shard_map/psum | solution.py:149
  1196.1 34.6 %all_gather.23 = f32[1024,64]{1,0:T(8,128)S(1)} all-gather(f32[8,64]{1,0:T(8,128)S(1)} %fusion.30), channel_id=1, replica_groups=mesh['sx'=16,'sy'=8] {'sx','sy'}, dimensions={0}, use_global_device_ids=true | all-gather | bytes 264192 | tf_op jit(solution)/shard_map/all_gather | solution.py:80
  1248.9 7.7 collective-permute-done.47
  1258.1 68.0 %psum.94 = f32[64]{0:T(128)S(1)} all-reduce(f32[64]{0:T(128)S(1)} %multiply_reduce_fusion), channel_id=1, replica_groups=mesh['sx'=16,'sy'=8] {'sx','sy'}, use_global_device_ids=true, to_apply=%region_27.28 | all-reduce | flops 64 | bytes 512 | tf_op jit(solution)/shard_map/psum | solution.py:136
  1346.9 7.3 collective-permute-done.51
  1357.0 68.1 %psum.95 = f32[64]{0:T(128)S(1)} all-reduce(f32[64]{0:T(128)S(1)} %fusion.48), channel_id=1, replica_groups=mesh['sx'=16,'sy'=8] {'sx','sy'}, use_global_device_ids=true, to_apply=%region_29.30 | all-reduce | flops 64 | bytes 512 | tf_op jit(solution)/shard_map/psum | solution.py:149
  (316 shorter events, 349.3 us)
Async XLA Ops:
  5.6 21.0 %all-to-all-start = ((s32[128,1,4]{2,1,0:T(1,128)}), s32[128,1,4]{2,1,0:T(1,128)S(1)}, u32[]{:S(2)}, u32[]{:S(2)}) async-start(s32[128,1,4]{2,1,0:T(1,128)} %bitcast.7), calls=%async_computation | async-start | bytes 131072 | tf_op jit(solution)/shard_map/all_to_all | solution.py:108
  26.6 14.0 all-to-all-start.1
  44.6 10.0 collective-permute-start.1
  45.9 9.7 collective-permute-start
  55.7 13.3 collective-permute-start.3
  58.4 11.7 collective-permute-start.2
  129.4 13.3 collective-permute-start.7
  132.6 11.3 collective-permute-start.6
  155.0 15.0 %collective-permute-start.11 = (bf16[3,1,64,2048]{3,2,1,0:T(8,128)(2,1)S(1)}, bf16[3,1,64,2048]{3,2,1,0:T(8,128)(2,1)S(1)}, u32[]{:S(2)}, u32[]{:S(2)}) collective-permute-start(bf16[3,1,64,2048]{3,2,1,0:T(8,128)(2,1)S(1)} %pad_maximum_fusion.2), channel_id=1, source_target_pairs={{1,0},{2,1},{3,2},{4,3},{5,4},{6,5},{7,6},{9,8},{10,9},{11,10},{12... | collective-permute-start | bytes 2359304 | tf_op jit(solution)/shard_map/ppermute | solution.py:27
  156.9 14.2 collective-permute-start.10
  296.2 13.3 collective-permute-start.15
  299.4 11.3 collective-permute-start.14
  393.5 13.5 collective-permute-start.19
  397.8 10.8 collective-permute-start.18
  521.2 9.6 collective-permute-start.21
  531.8 13.3 collective-permute-start.23
  535.0 11.3 collective-permute-start.22
  631.1 13.4 collective-permute-start.27
  635.3 10.8 collective-permute-start.26
  759.6 9.6 collective-permute-start.29
  770.2 13.3 collective-permute-start.31
  773.4 11.3 collective-permute-start.30
  867.7 13.4 collective-permute-start.35
  872.0 10.8 collective-permute-start.34
  1005.8 13.3 collective-permute-start.39
  1009.0 11.3 collective-permute-start.38
  1105.2 13.4 collective-permute-start.43
  1109.4 10.8 collective-permute-start.42
  1243.3 13.3 collective-permute-start.47
  1246.5 11.3 collective-permute-start.46
  1340.8 13.5 collective-permute-start.51
  1345.0 10.8 collective-permute-start.50
  (67 other events, 2811.7 us)
where the time goes:
time: 1440 us; the launch traced here: 1430 us
  blocking collectives  962 us (67%)
  waiting for transfers between devices  192 us (13%)
  starting transfers between devices  162 us (11%)
  matrix products  82.1 us (6%)
  other arithmetic  21.7 us (2%)
    psum x6, blocking collectives, products(): return lax.psum(jnp.sum(weight * left * right, axis=1), ('sx', 'sy'))  410 us
    psum x5, blocking collectives, body(): curv = lax.psum(curv_local, ('sx', 'sy'))  340 us
    all_gather x6, blocking collectives, gather_coarse(): return lax.all_gather(coarse_local, ('sx', 'sy'), axis=0, tiled=True)  211 us
    ppermute x26, waiting for transfers between devices, padded_2(): lax.ppermute(head, axis, [((i + 1) % count, i) for i in range(ends)])  147 us
    ppermute x26, starting transfers between devices, padded_2(): lax.ppermute(tail, axis, [(i, (i + 1) % count) for i in range(ends)])  84.7 us
    ppermute x26, starting transfers between devices, padded_2(): lax.ppermute(head, axis, [((i + 1) % count, i) for i in range(ends)])  61.6 us
    dot_general x6, matrix products, precond(): jnp.dot(scaled.astype(jnp.bfloat16), inverse_mat, preferred_element_type=...  29.9 us
    ppermute x26, waiting for transfers between devices, padded_2(): lax.ppermute(tail, axis, [(i, (i + 1) % count) for i in range(ends)])  29.6 us
  transfers between devices with their start and end apart: 54, of which 54 were waited for; matrix products, arithmetic and copies ran while one was open for 0% of the time, Pallas kernels for 0%

commit v1 on v0

v1 whole, which is shorter than its diff:
```python
import functools

import jax
import jax.numpy as jnp
from jax import lax
from jax.experimental import pallas as pl
from jax.experimental.pallas import tpu as pltpu
from jax.sharding import PartitionSpec as P

ITERS = 6
MESH = pl.DeviceIdType.MESH
F32 = jnp.float32
BF16 = jnp.bfloat16
HP = lax.Precision.HIGHEST
NT = (((1,), (1,)), ((), ()))


def split3(value):
    high = value.astype(BF16)
    rest = value - high.astype(F32)
    mid = rest.astype(BF16)
    low = (rest - mid.astype(F32)).astype(BF16)
    return jnp.concatenate([high, mid, low], axis=0)


def kernel(
    cols, rows,
    values_ref, dest_ref, node_ref, schur_hbm, inverse_hbm, coarse_ref,
    x_ref, r_ref,
    schur, inverse, obs_send, obs_mid, obs_got, k_send, k_got, k_stack,
    vec_b, d_ref, s_ref, z_ref, q_ref, sb_ref,
    lin_send, lin_got, sch_send, sch_got,
    pay1, got1, pay2, got2, state,
    mat_sem, obs_sem, k_sem, lin_sem, sch_sem, one_sem, two_sem, out_sem,
):
    a = lax.axis_index("sx")
    b = lax.axis_index("sy")
    size = schur.shape[0]
    edge = size // 4
    realiz = values_ref.shape[1]
    obs = values_ref.shape[0]
    count = coarse_ref.shape[1]
    per_col = 8 * rows

    def sx_peer(j):
        return (lax.rem(a + j, cols), b)

    def sy_peer(j):
        return (a, lax.rem(b + j, rows))

    barrier = pltpu.get_barrier_semaphore()
    for j in range(1, rows):
        pl.semaphore_signal(barrier, inc=1, device_id=sy_peer(j), device_id_type=MESH)
    for j in range(1, cols):
        pl.semaphore_signal(barrier, inc=1, device_id=sx_peer(j), device_id_type=MESH)

    load_inverse = pltpu.make_async_copy(inverse_hbm.at[0, 0], inverse, mat_sem.at[0])
    load_schur = pltpu.make_async_copy(schur_hbm.at[0, 0], schur, mat_sem.at[1])
    load_schur.start()
    load_inverse.start()

    nbr = (sx_peer(cols - 1), sx_peer(1), sy_peer(rows - 1), sy_peer(1))
    opposite = (1, 0, 3, 2)
    there = (a > 0, a < cols - 1, b > 0, b < rows - 1)
    mask = [jnp.where(t, 1.0, 0.0).astype(F32) for t in there]
    weight = [jnp.where(t, 0.5, 1.0).astype(F32) for t in there]
    span = [slice(e * edge, (e + 1) * edge) for e in range(4)]
    flat = 1.0 / float(edge) ** 0.5
    ramp_norm = (edge * (edge * edge - 1) / 12.0) ** 0.5
    ramp = (
        lax.broadcasted_iota(jnp.int32, (1, edge), 1).astype(F32) - (edge - 1) / 2.0
    ) * (1.0 / ramp_norm)

    target_col = dest_ref[...]
    target_row = jnp.transpose(
        jnp.broadcast_to(target_col.astype(F32), (obs, 128))
    )[0:1].astype(jnp.int32)
    first = lax.broadcasted_iota(jnp.int32, (obs, obs), 0)
    second = lax.broadcasted_iota(jnp.int32, (obs, obs), 1)
    earlier = jnp.where((target_col == target_row) & (first < second), 1.0, 0.0)
    slot_row = jnp.sum(earlier, axis=0, keepdims=True).astype(jnp.int32)
    place = (lax.rem(target_row, rows) * cols + target_row // rows) * 8 + slot_row
    node_col = jnp.transpose(
        jnp.broadcast_to(node_ref[...].astype(F32), (128, obs))
    ).astype(jnp.int32)
    lane = lax.broadcasted_iota(jnp.int32, (obs, 128), 1)
    wide = jnp.concatenate(
        [values_ref[...].astype(F32), jnp.zeros((obs, 128 - realiz), F32)], axis=1
    )
    row_data = jnp.where(
        lane == realiz,
        (node_col // 128).astype(F32),
        jnp.where(lane == realiz + 1, lax.rem(node_col, 128).astype(F32), wide),
    ).astype(BF16)
    for t in range(rows):
        part = cols * 8
        spot = lax.broadcasted_iota(jnp.int32, (part, obs), 0) + t * part
        pick = jnp.where(spot == place, 1.0, 0.0).astype(BF16)
        obs_send[t] = jnp.dot(pick, row_data, preferred_element_type=F32).reshape(
            cols, 8, 128
        )

    inv_rows = coarse_ref[...]
    index = lax.broadcasted_iota(jnp.int32, (8, count), 1)
    sub_col = index // per_col
    sub_row = lax.rem(index // 8, rows)
    side = lax.rem(index, 8) // 2
    shared = (
        ((side == 0) & (sub_col > 0))
        | ((side == 1) & (sub_col < cols - 1))
        | ((side == 2) & (sub_row > 0))
        | ((side == 3) & (sub_row < rows - 1))
    )
    from_west = pltpu.roll(inv_rows, per_col - 2, axis=1)
    from_east = pltpu.roll(inv_rows, count - (per_col - 2), axis=1)
    from_south = pltpu.roll(inv_rows, 6, axis=1)
    from_north = pltpu.roll(inv_rows, count - 6, axis=1)
    across = jnp.where(
        side == 0,
        from_west,
        jnp.where(side == 1, from_east, jnp.where(side == 2, from_south, from_north)),
    )
    combined = jnp.where(shared, 0.5 * (inv_rows + across), inv_rows)
    k_send[...] = jnp.zeros_like(k_send)
    for t in range(cols):
        k_send[t, :, 0:per_col] = combined[:, t * per_col : (t + 1) * per_col]

    state[...] = jnp.zeros_like(state)
    state[2] = jnp.ones_like(state[2])
    x_ref[...] = jnp.zeros_like(x_ref)
    d_ref[...] = jnp.zeros_like(d_ref)
    s_ref[...] = jnp.zeros_like(s_ref)

    pl.semaphore_wait(barrier, rows - 1 + cols - 1)

    for j in range(1, rows):
        pltpu.make_async_remote_copy(
            obs_send.at[lax.rem(b + j, rows)], obs_mid.at[j],
            obs_sem.at[0], obs_sem.at[1],
            device_id=sy_peer(j), device_id_type=MESH,
        ).start()
    for j in range(1, cols):
        pltpu.make_async_remote_copy(
            k_send.at[lax.rem(a + j, cols)], k_got.at[cols - j],
            k_sem.at[0], k_sem.at[1],
            device_id=sx_peer(j), device_id_type=MESH,
        ).start()
    obs_mid[0] = obs_send[b]
    k_got[0] = k_send[a]

    edge_of = lax.broadcasted_iota(jnp.int32, (8, size), 1) // edge
    offset = lax.rem(lax.broadcasted_iota(jnp.int32, (8, size), 1), edge).astype(F32)
    function = lax.broadcasted_iota(jnp.int32, (8, size), 0)
    basis = jnp.where(
        edge_of == function // 2,
        jnp.where(
            lax.rem(function, 2) == 0, flat, (offset - (edge - 1) / 2.0) * (1.0 / ramp_norm)
        ),
        0.0,
    ).astype(F32)
    basis3 = split3(basis)
    load_schur.wait()
    for e in range(4):
        made = jnp.dot(basis3, schur[:, span[e]], preferred_element_type=F32)
        sb_ref[:, span[e]] = split3(made[0:8] + made[8:16] + made[16:24])

    def wait_bytes(ref, sem):
        pltpu.make_async_copy(ref, ref, sem).wait()

    wait_bytes(obs_mid.at[pl.ds(1, rows - 1)], obs_sem.at[1])
    wait_bytes(obs_mid.at[pl.ds(1, rows - 1)], obs_sem.at[0])
    for j in range(1, cols):
        pltpu.make_async_remote_copy(
            obs_mid.at[:, lax.rem(a + j, cols)], obs_got.at[j],
            obs_sem.at[2], obs_sem.at[3],
            device_id=sx_peer(j), device_id_type=MESH,
        ).start()
    obs_got[0] = obs_mid[:, a]
    wait_bytes(k_got.at[pl.ds(1, cols - 1)], k_sem.at[1])
    wait_bytes(k_got.at[pl.ds(1, cols - 1)], k_sem.at[0])
    k_stack[...] = k_got[...].reshape(cols * 8, 128)
    wait_bytes(obs_got.at[pl.ds(1, cols - 1)], obs_sem.at[3])
    wait_bytes(obs_got.at[pl.ds(1, cols - 1)], obs_sem.at[2])

    got = obs_got[...].reshape(cols * rows * 8, 128)
    got_node = (got[:, realiz : realiz + 1] * 128.0 + got[:, realiz + 1 : realiz + 2])
    got_node = got_node.astype(jnp.int32)
    got_values = jnp.transpose(got)[0:realiz].astype(BF16)

    def sch_copy(e):
        return pltpu.make_async_remote_copy(
            sch_send.at[e], sch_got.at[opposite[e]],
            sch_sem.at[0, e], sch_sem.at[1, opposite[e]],
            device_id=nbr[e], device_id_type=MESH,
        )

    def lin_copy(e):
        return pltpu.make_async_remote_copy(
            lin_send.at[e], lin_got.at[opposite[e]],
            lin_sem.at[0, e], lin_sem.at[1, opposite[e]],
            device_id=nbr[e], device_id_type=MESH,
        )

    for e in range(4):
        at = lax.broadcasted_iota(jnp.int32, (cols * rows * 8, edge), 1) + e * edge
        hot = jnp.where(at == got_node, 1.0, 0.0).astype(BF16)
        q_ref[:, span[e]] = jnp.dot(got_values, hot, preferred_element_type=F32)
        sch_send[e] = q_ref[:, span[e]].astype(BF16)
        sch_copy(e).start()

    def global_round(parity):
        for j in range(1, rows):
            pltpu.make_async_remote_copy(
                pay1, got1.at[parity, b], out_sem.at[0], one_sem.at[parity],
                device_id=sy_peer(j), device_id_type=MESH,
            ).start()
        got1[parity, b] = pay1[...]
        wait_bytes(got1.at[parity, pl.ds(0, rows - 1)], one_sem.at[parity])
        wait_bytes(got1.at[parity, pl.ds(0, rows - 1)], out_sem.at[0])
        gathered = got1[parity]
        stack = gathered.reshape(rows * 8, 128)
        partial = jnp.dot(
            k_stack[:, 0:per_col], stack, precision=HP, preferred_element_type=F32
        )
        sums = jnp.sum(gathered, axis=0)
        left = lax.broadcasted_iota(jnp.int32, (8, 128), 1) < realiz
        for j in range(cols):
            pay2[j] = jnp.where(left, partial[j * 8 : (j + 1) * 8], sums)
        for j in range(1, cols):
            pltpu.make_async_remote_copy(
                pay2.at[j], got2.at[parity, j], out_sem.at[1], two_sem.at[parity],
                device_id=sx_peer(j), device_id_type=MESH,
            ).start()
        got2[parity, 0] = pay2[0]
        wait_bytes(got2.at[parity, pl.ds(1, cols - 1)], two_sem.at[parity])
        wait_bytes(got2.at[parity, pl.ds(1, cols - 1)], out_sem.at[1])
        return jnp.transpose(jnp.sum(got2[parity], axis=0))

    start_coarse = lax.dot_general(
        basis, q_ref[...], NT, precision=HP, preferred_element_type=F32
    )
    pay1[...] = jnp.concatenate([start_coarse, jnp.zeros((8, 128 - realiz), F32)], axis=1)
    total = global_round(1)
    state[0, :, 0:8] = total[0:realiz]
    for e in range(4):
        sch_copy(e).wait_send()
        sch_copy(opposite[e]).wait_recv()
        r_ref[:, span[e]] = q_ref[:, span[e]] + mask[e] * sch_got[e].astype(F32)
    load_inverse.wait()

    def step(k, carry):
        parity = lax.rem(k, 2)
        coarse = state[0]
        for e in range(4):
            vec_b[:, span[e]] = (weight[e] * r_ref[:, span[e]]).astype(BF16)
        sum_rq = jnp.zeros((realiz, 128), F32)
        for e in range(4):
            part = jnp.dot(vec_b[...], inverse[:, span[e]], preferred_element_type=F32)
            fix = coarse[:, 2 * e : 2 * e + 1] * flat + coarse[:, 2 * e + 1 : 2 * e + 2] * ramp
            local = weight[e] * (part + fix)
            lin_send[e] = local.astype(BF16)
            lin_copy(e).start()
            q_ref[:, span[e]] = local
            prod = local * r_ref[:, span[e]]
            for t in range(edge // 128):
                sum_rq += prod[:, t * 128 : (t + 1) * 128]
        sum_zs = jnp.zeros((realiz, 128), F32)
        for e in (2, 3, 0, 1):
            lin_copy(e).wait_send()
            lin_copy(opposite[e]).wait_recv()
            z = q_ref[:, span[e]] + mask[e] * lin_got[e].astype(F32)
            z_ref[:, span[e]] = z
            vec_b[:, span[e]] = z.astype(BF16)
            prod = (weight[e] * z) * s_ref[:, span[e]]
            for t in range(edge // 128):
                sum_zs += prod[:, t * 128 : (t + 1) * 128]
        sum_zy = jnp.zeros((realiz, 128), F32)
        for e in range(4):
            y = jnp.dot(vec_b[...], schur[:, span[e]], preferred_element_type=F32)
            sch_send[e] = y.astype(BF16)
            sch_copy(e).start()
            q_ref[:, span[e]] = y
            prod = z_ref[:, span[e]] * y
            for t in range(edge // 128):
                sum_zy += prod[:, t * 128 : (t + 1) * 128]
        made = lax.dot_general(sb_ref[...], vec_b[...], NT, preferred_element_type=F32)
        local_coarse = made[0:8] + made[8:16] + made[16:24]
        lane = lax.broadcasted_iota(jnp.int32, (realiz, 128), 1)
        dots = jnp.where(
            lane == 0,
            jnp.sum(sum_rq, axis=1, keepdims=True),
            jnp.where(
                lane == 1,
                jnp.sum(sum_zy, axis=1, keepdims=True),
                jnp.where(lane == 2, jnp.sum(sum_zs, axis=1, keepdims=True), 0.0),
            ),
        )
        pay1[...] = jnp.concatenate([local_coarse, jnp.transpose(dots)[0:8]], axis=1)
        total = global_round(parity)
        made_coarse = total[0:realiz]
        sums = total[realiz : 2 * realiz]
        rz = sums[:, 0:1]
        rz_old = state[2, :, 0:1]
        curv_old = state[3, :, 0:1]
        beta = rz / rz_old
        curv = sums[:, 1:2] + 2.0 * beta * sums[:, 2:3] + beta * beta * curv_old
        alpha = rz / curv
        state[2] = jnp.broadcast_to(rz, (realiz, 128))
        state[3] = jnp.broadcast_to(curv, (realiz, 128))
        image_coarse = made_coarse + beta * state[1, :, 0:8]
        state[1, :, 0:8] = image_coarse
        state[0, :, 0:8] = state[0, :, 0:8] - alpha * image_coarse
        for e in range(4):
            sch_copy(e).wait_send()
            sch_copy(opposite[e]).wait_recv()
            image = (
                q_ref[:, span[e]]
                + mask[e] * sch_got[e].astype(F32)
                + beta * s_ref[:, span[e]]
            )
            s_ref[:, span[e]] = image
            direction = z_ref[:, span[e]] + beta * d_ref[:, span[e]]
            d_ref[:, span[e]] = direction
            x_ref[:, span[e]] = x_ref[:, span[e]] + alpha * direction
            r_ref[:, span[e]] = r_ref[:, span[e]] - alpha * image
        return carry

    lax.fori_loop(0, ITERS, step, 0)


def body(cols, rows, obs_values, obs_dest, obs_node, schur, local_inverse, coarse_inverse):
    size = schur.shape[-1]
    edge = size // 4
    realiz = obs_values.shape[1]
    obs = obs_values.shape[0]
    vmem = pl.BlockSpec(memory_space=pltpu.VMEM)
    hbm = pl.BlockSpec(memory_space=pl.ANY)
    vector = pltpu.VMEM((realiz, size), F32)
    halo = pltpu.VMEM((4, realiz, edge), BF16)
    out = jax.ShapeDtypeStruct((realiz, size), F32)
    dma = pltpu.SemaphoreType.DMA
    found, residual = pl.pallas_call(
        functools.partial(kernel, cols, rows),
        out_shape=(out, out),
        in_specs=[vmem, vmem, vmem, hbm, hbm, vmem],
        out_specs=(vmem, vmem),
        scratch_shapes=[
            pltpu.VMEM((size, size), BF16),
            pltpu.VMEM((size, size), BF16),
            pltpu.VMEM((rows, cols, 8, 128), F32),
            pltpu.VMEM((rows, cols, 8, 128), F32),
            pltpu.VMEM((cols, rows, 8, 128), F32),
            pltpu.VMEM((cols, 8, 128), F32),
            pltpu.VMEM((cols, 8, 128), F32),
            pltpu.VMEM((cols * 8, 128), F32),
            pltpu.VMEM((realiz, size), BF16),
            vector, vector, vector, vector,
            pltpu.VMEM((24, size), BF16),
            halo, halo, halo, halo,
            pltpu.VMEM((8, 128), F32),
            pltpu.VMEM((2, rows, 8, 128), F32),
            pltpu.VMEM((cols, 8, 128), F32),
            pltpu.VMEM((2, cols, 8, 128), F32),
            pltpu.VMEM((4, realiz, 128), F32),
            dma((2,)), dma((4,)), dma((2,)), dma((2, 4)), dma((2, 4)),
            dma((2,)), dma((2,)), dma((2,)),
        ],
        compiler_params=pltpu.CompilerParams(
            collective_id=0, has_side_effects=True, vmem_limit_bytes=48 << 20
        ),
    )(obs_values, obs_dest, obs_node.reshape(1, obs), schur, local_inverse, coarse_inverse)
    return found[None, None], residual[None, None]


def solution(mesh):
    placed = (
        P(("sx", "sy"), None),
        P(("sx", "sy"), None),
        P(("sx", "sy")),
        P("sx", "sy", None, None),
        P("sx", "sy", None, None),
        P(("sx", "sy"), None),
    )
    return jax.shard_map(
        functools.partial(body, mesh.shape["sx"], mesh.shape["sy"]),
        mesh=mesh,
        in_specs=placed,
        out_specs=(P("sx", "sy", None, None), P("sx", "sy", None, None)),
        check_vma=False,
    )
```

time: 1440 us -> 142 us (0.10)
  blocking collectives: 962 us -> 0 us
  waiting for transfers between devices: 192 us -> 0 us
  starting transfers between devices: 162 us -> 0 us
  Pallas kernels: 0 us -> 136 us
  matrix products: 82.1 us -> 0 us
  other arithmetic: 21.7 us -> 0 us
    psum x11 -> x0, blocking collectives: 750 us -> none  [the longest x6 410 us: products(): return lax.psum(jnp.sum(weight * left * right, axis=1), ('sx', 'sy'))]
    all_gather x6 -> x0, blocking collectives: 211 us -> none  [gather_coarse(): return lax.all_gather(coarse_local, ('sx', 'sy'), axis=0, tiled=True)]
    ppermute x52 -> x0, waiting for transfers between devices: 177 us -> none  [the longest x26 147 us: padded_2(): lax.ppermute(head, axis, [((i + 1) % count, i) for i in range(ends)])]
    ppermute x52 -> x0, starting transfers between devices: 146 us -> none  [the longest x26 84.7 us: padded_2(): lax.ppermute(tail, axis, [(i, (i + 1) % count) for i in range(ends)])]
    pallas_call x0 -> x1, Pallas kernels: none -> 136 us  [body(): pl.pallas_call(functools.partial(kernel, cols, rows), out_shape=(out, out...]
    dot_general x30 -> x0, matrix products: 82.1 us -> none  [the longest x6 29.9 us: precond(): jnp.dot(scaled.astype(jnp.bfloat16), inverse_mat, preferred_element_type=...]
    all_to_all x2 -> x0, starting transfers between devices: 16 us -> none  [the longest x1 11.5 us: body(): lax.all_to_all(send_nodes.reshape(dev_count, capacity), ('sx', 'sy'), spl...]
    all_to_all x2 -> x0, waiting for transfers between devices: 14.8 us -> none  [the longest x1 8.1 us: body(): lax.all_to_all(send_values.reshape(dev_count, capacity, realiz), ('sx', '...]
  transfers between devices with their start and end apart: 54 -> 0, of which waited for: 54 -> 0; matrix products, arithmetic and copies ran while one was open for 0% -> 0% of each run, Pallas kernels for 0% -> 0%
where the time goes in v1:
time: 142 us
  Pallas kernels  136 us (96%)
  local copies, waits for them, and re-layouts  4.71 us (3%)
    pallas_call x1, Pallas kernels, body(): pl.pallas_call(functools.partial(kernel, cols, rows), out_shape=(out, out...  136 us
    unnamed x8, local copies, waits for them, and re-layouts  4.71 us

profile of v1, /device:TPU:1, one launch (start us, length us, event | category | flops | bytes accessed | tf_op | source)
XLA Modules:
  0.0 141.5 jit_solution(5123325774484745930)
XLA Ops:
  0.6 0.9 copy.8.values_ref
  1.5 0.8 copy.9.dest_ref
  2.3 0.0 copy-start
  2.3 0.8 copy-done
  3.1 0.0 copy-start.1
  3.1 0.7 copy-done.1
  3.8 136.2 %shard_map.77 = (f32[64,2048]{1,0:T(8,128)S(1)}, f32[64,2048]{1,0:T(8,128)S(1)}) custom-call(bf16[256,64]{1,0:T(8,128)(2,1)S(1)} %copy.8.values_ref, s32[256,1]{1,0:T(8,128)S(1)} %copy.9.dest_ref, s32[1,256]{1,0:T(1,128)S(1)} %bitcast.5, bf16[1,1,2048,2048]{3,2,1,0:T(8,128)(2,1)} %schur_hbm.1, bf16[1,1,2048,2048]{3,2,1,0:T(8,128)(2,1)} %inverse_hbm.1, ...), custom_call_target="tpu_custom_call" | custom-call | tf_op jit(solution)/shard_map/pallas_call | solution.py:342
  139.9 0.8 copy.12
  140.7 0.8 copy.13
Async XLA Ops:
  2.3 0.8 copy-start
  3.1 0.7 copy-start.1

commit v2 on v1

v2 whole, which is shorter than its diff:
```python
import functools

import jax
import jax.numpy as jnp
from jax import lax
from jax.experimental import pallas as pl
from jax.experimental.pallas import tpu as pltpu
from jax.sharding import PartitionSpec as P

ITERS = 6
MESH = pl.DeviceIdType.MESH
F32 = jnp.float32
BF16 = jnp.bfloat16
NT = (((1,), (1,)), ((), ()))


def split(value, parts):
    found = []
    for _ in range(parts):
        piece = value.astype(BF16)
        found.append(piece)
        value = value - piece.astype(F32)
    return found


def wait_bytes(ref, sem):
    pltpu.make_async_copy(ref, ref, sem).wait()


def kernel(
    cols, rows,
    values_hbm, dest_hbm, node_hbm, schur_hbm, inverse_hbm, coarse_hbm,
    x_ref, r_ref,
    values_ref, dest_ref, node_ref, coarse_ref, schur, inverse,
    obs_send, obs_mid, obs_got, k_send, k_got, k_row, k_side, k_cat,
    zb_ref, yb_ref, d_ref, s_ref, t_ref, z_ref, y_ref, h_ref, sb_ref,
    lin_send, lin_got, sch_send, sch_got,
    pay1, got1, pay2, got2, state, late_ref,
    in_sem, mat_sem, obs_sem, k_sem, side_sem, lin_sem, sch_sem, one_sem, two_sem, out_sem,
):
    a = lax.axis_index("sx")
    b = lax.axis_index("sy")
    size = schur.shape[0]
    edge = size // 4
    realiz = values_ref.shape[0]
    obs = values_ref.shape[1]
    count = coarse_ref.shape[1]
    per_col = 8 * rows
    chips = rows // 2

    def sx_peer(j):
        return (lax.rem(a + j, cols), b)

    def sy_peer(j):
        return (a, lax.rem(b + j, rows))

    small = [
        pltpu.make_async_copy(dest_hbm, dest_ref, in_sem.at[0]),
        pltpu.make_async_copy(node_hbm, node_ref, in_sem.at[1]),
        pltpu.make_async_copy(values_hbm, values_ref, in_sem.at[2]),
        pltpu.make_async_copy(coarse_hbm, coarse_ref, in_sem.at[3]),
    ]
    for copy in small:
        copy.start()
    barrier = pltpu.get_barrier_semaphore()
    for j in range(1, cols):
        pl.semaphore_signal(barrier, inc=1, device_id=sx_peer(j), device_id_type=MESH)
    for j in range(1, rows):
        pl.semaphore_signal(barrier, inc=1, device_id=sy_peer(j), device_id_type=MESH)
    load_schur = pltpu.make_async_copy(schur_hbm.at[0, 0], schur, mat_sem.at[1])
    load_inverse = pltpu.make_async_copy(inverse_hbm.at[0, 0], inverse, mat_sem.at[0])
    load_schur.start()
    load_inverse.start()

    nbr = (sx_peer(cols - 1), sx_peer(1), sy_peer(rows - 1), sy_peer(1))
    opposite = (1, 0, 3, 2)
    there = (a > 0, a < cols - 1, b > 0, b < rows - 1)
    mask = [jnp.where(t, 1.0, 0.0).astype(F32) for t in there]
    weight = [jnp.where(t, 0.5, 1.0).astype(F32) for t in there]
    span = [slice(e * edge, (e + 1) * edge) for e in range(4)]
    flat = 1.0 / float(edge) ** 0.5
    ramp_norm = (edge * (edge * edge - 1) / 12.0) ** 0.5
    ramp = (
        lax.broadcasted_iota(jnp.int32, (1, edge), 1).astype(F32) - (edge - 1) / 2.0
    ) * (1.0 / ramp_norm)

    small[0].wait()
    target_row = dest_ref[...]
    target_col = jnp.transpose(
        jnp.broadcast_to(target_row.astype(F32), (128, obs))
    )[:, 0:1].astype(jnp.int32)
    first = lax.broadcasted_iota(jnp.int32, (obs, obs), 0)
    second = lax.broadcasted_iota(jnp.int32, (obs, obs), 1)
    earlier = jnp.where((target_col == target_row) & (first < second), 1.0, 0.0)
    slot_row = jnp.sum(earlier, axis=0, keepdims=True).astype(jnp.int32)
    place = target_row * 4 + slot_row
    small[1].wait()
    small[2].wait()
    node = node_ref[...]
    below = lax.broadcasted_iota(jnp.int32, (128 - realiz, obs), 0)
    tail = jnp.where(
        below == 0,
        (node // 128).astype(F32),
        jnp.where(below == 1, lax.rem(node, 128).astype(F32), 0.0),
    )
    row_data = jnp.concatenate([values_ref[...], tail.astype(BF16)], axis=0)
    for t in range(4):
        part = cols * rows
        spot = lax.broadcasted_iota(jnp.int32, (part, obs), 0) + t * part
        pick = jnp.where(spot == place, 1.0, 0.0).astype(BF16)
        made = lax.dot_general(pick, row_data, NT, preferred_element_type=F32)
        obs_send[t * cols // 4 : (t + 1) * cols // 4] = made.reshape(
            cols // 4, chips, 8, 128
        ).astype(BF16)

    pl.semaphore_wait(barrier, rows - 1 + cols - 1)

    for j in range(1, cols):
        pltpu.make_async_remote_copy(
            obs_send.at[lax.rem(a + j, cols)], obs_mid.at[j],
            obs_sem.at[0], obs_sem.at[1],
            device_id=sx_peer(j), device_id_type=MESH,
        ).start()
    obs_mid[0] = obs_send[a]

    small[3].wait()
    inv_rows = coarse_ref[...]
    index = lax.broadcasted_iota(jnp.int32, (8, count), 1)
    sub_col = index // per_col
    sub_row = lax.rem(index // 8, rows)
    side = lax.rem(index, 8) // 2
    shared = (
        ((side == 0) & (sub_col > 0))
        | ((side == 1) & (sub_col < cols - 1))
        | ((side == 2) & (sub_row > 0))
        | ((side == 3) & (sub_row < rows - 1))
    )
    from_west = pltpu.roll(inv_rows, per_col - 2, axis=1)
    from_east = pltpu.roll(inv_rows, count - (per_col - 2), axis=1)
    from_south = pltpu.roll(inv_rows, 6, axis=1)
    from_north = pltpu.roll(inv_rows, count - 6, axis=1)
    across = jnp.where(
        side == 0,
        from_west,
        jnp.where(side == 1, from_east, jnp.where(side == 2, from_south, from_north)),
    )
    combined = jnp.where(shared, 0.5 * (inv_rows + across), inv_rows)
    k_send[...] = jnp.zeros_like(k_send)
    for t in range(cols):
        k_send[t, :, 0:per_col] = combined[:, t * per_col : (t + 1) * per_col]
    for j in range(1, cols):
        pltpu.make_async_remote_copy(
            k_send.at[lax.rem(a + j, cols)], k_got.at[cols - j],
            k_sem.at[0], k_sem.at[1],
            device_id=sx_peer(j), device_id_type=MESH,
        ).start()
    k_got[0] = k_send[a]

    wait_bytes(obs_mid.at[pl.ds(1, cols - 1)], obs_sem.at[1])
    for j in range(1, rows):
        pltpu.make_async_remote_copy(
            obs_mid.at[:, lax.rem(b + j, rows) // 2], obs_got.at[j],
            obs_sem.at[2], obs_sem.at[3],
            device_id=sy_peer(j), device_id_type=MESH,
        ).start()
    obs_got[0] = obs_mid[:, b // 2]

    wait_bytes(k_got.at[pl.ds(1, cols - 1)], k_sem.at[1])
    k_row[...] = k_got[...].reshape(cols * 8, 128)
    side_copy = [
        pltpu.make_async_remote_copy(
            k_row, k_side.at[i], side_sem.at[0, i], side_sem.at[1, i],
            device_id=sy_peer(step), device_id_type=MESH,
        )
        for i, step in ((0, 1), (1, rows - 1))
    ]
    for copy in side_copy:
        copy.start()

    edge_of = lax.broadcasted_iota(jnp.int32, (8, size), 1) // edge
    offset = lax.rem(lax.broadcasted_iota(jnp.int32, (8, size), 1), edge).astype(F32)
    function = lax.broadcasted_iota(jnp.int32, (8, size), 0)
    basis = jnp.where(
        edge_of == function // 2,
        jnp.where(
            lax.rem(function, 2) == 0, flat, (offset - (edge - 1) / 2.0) * (1.0 / ramp_norm)
        ),
        0.0,
    ).astype(F32)
    basis3 = jnp.concatenate(split(basis, 3), axis=0)
    load_schur.wait()
    for e in range(4):
        made = jnp.dot(basis3, schur[:, span[e]], preferred_element_type=F32)
        sb_ref[:, span[e]] = jnp.concatenate(
            split(made[0:8] + made[8:16] + made[16:24], 2), axis=0
        )
    state[0] = jnp.ones_like(state[0])
    state[1] = jnp.zeros_like(state[1])
    x_ref[...] = jnp.zeros_like(x_ref)
    d_ref[...] = jnp.zeros_like(d_ref)
    s_ref[...] = jnp.zeros_like(s_ref)
    t_ref[...] = jnp.zeros_like(t_ref)
    pay1[...] = jnp.zeros_like(pay1)

    wait_bytes(obs_got.at[pl.ds(1, rows - 1)], obs_sem.at[3])
    got = obs_got[...].astype(F32).reshape(cols * rows * 8, 128)
    own_half = lax.rem(lax.broadcasted_iota(jnp.int32, (cols * rows * 8, 1), 0), 8) // 4
    got_node = got[:, realiz : realiz + 1] * 128.0 + got[:, realiz + 1 : realiz + 2]
    got_node = jnp.where(own_half == lax.rem(b, 2), got_node.astype(jnp.int32), -1)
    got_values = jnp.transpose(got)[0:realiz].astype(BF16)

    def sch_copy(i, parity=0):
        e, part = i % 4, i // 4
        at = opposite[e] + 4 * part * (1 + parity)
        return pltpu.make_async_remote_copy(
            sch_send.at[i], sch_got.at[at], sch_sem.at[0, i], sch_sem.at[1, at],
            device_id=nbr[e], device_id_type=MESH,
        )

    def lin_copy(i, parity=0):
        e, part = i % 4, i // 4
        at = opposite[e] + 4 * part * (1 + parity)
        return pltpu.make_async_remote_copy(
            lin_send.at[i], lin_got.at[at], lin_sem.at[0, i], lin_sem.at[1, at],
            device_id=nbr[e], device_id_type=MESH,
        )

    def send_partial(e, y):
        y_ref[:, span[e]] = y
        high, low = split(y, 2)
        sch_send[e] = high
        sch_copy(e).start()
        sch_send[4 + e] = low

    def send_payload(parity):
        for j in range(1, rows):
            pltpu.make_async_remote_copy(
                pay1, got1.at[parity, b], out_sem.at[0], one_sem.at[parity],
                device_id=sy_peer(j), device_id_type=MESH,
            ).start()
        got1[parity, b] = pay1[...]
        for e in range(4):
            sch_copy(4 + e, parity).start()

    def pass_payload(parity):
        wait_bytes(got1.at[parity, pl.ds(0, rows - 1)], one_sem.at[parity])
        wait_bytes(got1.at[parity, pl.ds(0, rows - 1)], out_sem.at[0])
        gathered = got1[parity]
        high, low = split(gathered.reshape(rows * 8, 128), 2)
        stack = jnp.concatenate([high, low, high], axis=0)
        partial = jnp.dot(k_cat[...], stack, preferred_element_type=F32)
        sums = jnp.sum(gathered, axis=0)
        left = lax.broadcasted_iota(jnp.int32, (8, 128), 1) < realiz
        for j in range(1, cols):
            pay2[j] = jnp.where(left, partial[j * 8 : (j + 1) * 8], sums)
            pltpu.make_async_remote_copy(
                pay2.at[j], got2.at[parity, j], out_sem.at[1], two_sem.at[parity],
                device_id=sx_peer(j), device_id_type=MESH,
            ).start()
        got2[parity, 0] = jnp.where(left, partial[0:8], sums)

    def take_payload(parity):
        wait_bytes(got2.at[parity, pl.ds(1, cols - 1)], two_sem.at[parity])
        wait_bytes(got2.at[parity, pl.ds(1, cols - 1)], out_sem.at[1])
        return jnp.transpose(jnp.sum(got2[parity], axis=0))

    def finish_image(e, parity):
        sch_copy(4 + e, parity).wait_send()
        sch_copy(4 + opposite[e], parity).wait_recv()
        return y_ref[:, span[e]] + mask[e] * sch_got[4 + 4 * parity + e].astype(F32)

    def take_high(e):
        sch_copy(e).wait_send()
        sch_copy(opposite[e]).wait_recv()
        y_ref[:, span[e]] = y_ref[:, span[e]] + mask[e] * sch_got[e].astype(F32)

    def put_y(e):
        high, low = split(weight[e] * y_ref[:, span[e]], 2)
        yb_ref[0:realiz, span[e]] = high
        yb_ref[realiz:, span[e]] = low

    def apply_inverse(parity):
        for e in (2, 3):
            take_high(e)
            y_ref[:, span[e]] = finish_image(e, parity)
            put_y(e)
        pass_payload(parity)
        for e in (0, 1):
            take_high(e)
            put_y(e)
        for e in range(4):
            made = jnp.dot(yb_ref[...], inverse[:, span[e]], preferred_element_type=F32)
            local = weight[e] * (made[0:realiz] + made[realiz:])
            high, low = split(local, 2)
            lin_send[e] = high
            lin_copy(e).start()
            lin_send[4 + e] = low
            h_ref[:, span[e]] = local
        for e in range(4):
            lin_copy(4 + e, parity).start()

    def coarse_part(e, total):
        return (
            total[0:realiz, 2 * e : 2 * e + 1] * flat
            + total[0:realiz, 2 * e + 1 : 2 * e + 2] * ramp
        )

    def take_lin(e):
        lin_copy(e).wait_send()
        lin_copy(opposite[e]).wait_recv()
        return mask[e] * lin_got[e].astype(F32)

    def take_low(e, alpha, once, parity):
        lin_copy(4 + e, parity).wait_send()
        lin_copy(4 + opposite[e], parity).wait_recv()
        low = mask[e] * lin_got[4 + 4 * parity + e].astype(F32)
        t_ref[:, span[e]] = t_ref[:, span[e]] + once * low
        late_ref[:, span[e]] = alpha * low

    def put_z(e, z):
        z_ref[:, span[e]] = z
        high, low = split(z, 2)
        zb_ref[0:realiz, span[e]] = high
        zb_ref[realiz:, span[e]] = low

    for e in range(4):
        at = lax.broadcasted_iota(jnp.int32, (cols * rows * 8, edge), 1) + e * edge
        hot = jnp.where(at == got_node, 1.0, 0.0).astype(BF16)
        send_partial(e, jnp.dot(got_values, hot, preferred_element_type=F32))
    loads = jnp.concatenate(split(y_ref[...], 2), axis=0)
    made = lax.dot_general(basis3, loads, NT, preferred_element_type=F32)
    made = made[0:8] + made[8:16] + made[16:24]
    pay1[:, 0:realiz] = made[:, 0:realiz] + made[:, realiz:]
    send_payload(1)

    for copy in side_copy:
        copy.wait_recv()
    rows_here = k_row[...]
    line = lax.broadcasted_iota(jnp.int32, (cols * 8, 1), 0)
    where_to = lax.rem(line // 8 + a, cols)
    line_side = lax.rem(line, 8) // 2
    k_west = jnp.where(where_to > 0, pltpu.roll(rows_here, 6, axis=0), 0.0)
    k_east = jnp.where(
        where_to < cols - 1, pltpu.roll(rows_here, cols * 8 - 6, axis=0), 0.0
    )
    k_south = mask[2] * pltpu.roll(k_side[0], cols * 8 - 2, axis=0)
    k_north = mask[3] * pltpu.roll(k_side[1], 2, axis=0)
    scale = jnp.where(
        line_side == 0,
        jnp.where(where_to > 0, 0.5, 1.0),
        jnp.where(
            line_side == 1,
            jnp.where(where_to < cols - 1, 0.5, 1.0),
            jnp.where(line_side == 2, weight[2], weight[3]),
        ),
    )
    rows_across = jnp.where(
        line_side == 0,
        k_west,
        jnp.where(line_side == 1, k_east, jnp.where(line_side == 2, k_south, k_north)),
    )
    k_high, k_low = split((scale * (rows_here + rows_across))[:, 0:per_col], 2)
    k_cat[...] = jnp.concatenate([k_high, k_high, k_low], axis=1)
    load_inverse.wait()

    apply_inverse(1)
    for e in (0, 1):
        r_ref[:, span[e]] = finish_image(e, 1)
    for e in (2, 3):
        r_ref[:, span[e]] = y_ref[:, span[e]]
    total = take_payload(1)
    for e in (2, 3, 0, 1):
        put_z(e, h_ref[:, span[e]] + coarse_part(e, total) + take_lin(e))
    state[2] = -jnp.ones_like(state[2])

    def apply_schur(parity):
        sum_rz = jnp.zeros((realiz, 128), F32)
        sum_zy = jnp.zeros((realiz, 128), F32)
        sum_zs = jnp.zeros((realiz, 128), F32)
        for e in range(4):
            made = jnp.dot(zb_ref[...], schur[:, span[e]], preferred_element_type=F32)
            y = made[0:realiz] + made[realiz:]
            send_partial(e, y)
            z = z_ref[:, span[e]]
            zw = weight[e] * z
            zy, zs, rz = z * y, zw * s_ref[:, span[e]], zw * r_ref[:, span[e]]
            for t in range(edge // 128):
                tile = slice(t * 128, (t + 1) * 128)
                sum_rz += rz[:, tile]
                sum_zy += zy[:, tile]
                sum_zs += zs[:, tile]
        made = lax.dot_general(sb_ref[...], zb_ref[...], NT, preferred_element_type=F32)
        made = made[0:8] + made[8:16]
        pay1[:, 0:realiz] = made[:, 0:realiz] + made[:, realiz:]
        lane = lax.broadcasted_iota(jnp.int32, (realiz, 128), 1)
        dots = jnp.where(
            lane == 0,
            jnp.sum(sum_rz, axis=1, keepdims=True),
            jnp.where(
                lane == 1,
                jnp.sum(sum_zy, axis=1, keepdims=True),
                jnp.where(lane == 2, jnp.sum(sum_zs, axis=1, keepdims=True), 0.0),
            ),
        )
        pay1[:, realiz:] = jnp.transpose(dots)[0:8]
        send_payload(parity)

    def factors(total):
        sums = total[realiz : 2 * realiz]
        rz = sums[:, 0:1]
        beta = rz / state[0, :, 0:1]
        curv = sums[:, 1:2] + beta * (2.0 * sums[:, 2:3] + beta * state[1, :, 0:1])
        state[0] = jnp.broadcast_to(rz, (realiz, 128))
        state[1] = jnp.broadcast_to(curv, (realiz, 128))
        state[2] = jnp.broadcast_to(rz / curv, (realiz, 128))
        return rz / curv, beta

    def advance(e, alpha, beta):
        image = y_ref[:, span[e]] + beta * s_ref[:, span[e]]
        s_ref[:, span[e]] = image
        direction = z_ref[:, span[e]] + beta * d_ref[:, span[e]]
        d_ref[:, span[e]] = direction
        x_ref[:, span[e]] = x_ref[:, span[e]] + alpha * direction
        r_ref[:, span[e]] = r_ref[:, span[e]] - alpha * image

    def step(k, carry):
        parity = lax.rem(k, 2)
        apply_schur(parity)
        for e in range(4):
            take_low(e, state[2, :, 0:1], jnp.where(k > 0, 1.0, 0.0).astype(F32), 1 - parity)
        apply_inverse(parity)
        for e in (0, 1):
            y_ref[:, span[e]] = finish_image(e, parity)
        total = take_payload(parity)
        alpha, beta = factors(total)
        for e in range(4):
            advance(e, alpha, beta)
            z_ref[:, span[e]] = z_ref[:, span[e]] - late_ref[:, span[e]]
            moved = h_ref[:, span[e]] + coarse_part(e, total) + beta * t_ref[:, span[e]]
            t_ref[:, span[e]] = moved
            z_ref[:, span[e]] = z_ref[:, span[e]] - alpha * moved
        for e in (2, 3, 0, 1):
            came = take_lin(e)
            t_ref[:, span[e]] = t_ref[:, span[e]] + came
            put_z(e, z_ref[:, span[e]] - alpha * came)
        return carry

    lax.fori_loop(0, ITERS - 1, step, 0)
    last = (ITERS - 1) % 2
    apply_schur(last)
    for e in range(4):
        lin_copy(4 + e, 1 - last).wait_send()
        lin_copy(4 + opposite[e], 1 - last).wait_recv()
    pass_payload(last)
    for e in range(4):
        take_high(e)
        y_ref[:, span[e]] = finish_image(e, last)
    alpha, beta = factors(take_payload(last))
    for e in range(4):
        advance(e, alpha, beta)

    wait_bytes(obs_mid.at[pl.ds(1, cols - 1)], obs_sem.at[0])
    wait_bytes(obs_got.at[pl.ds(1, rows - 1)], obs_sem.at[2])
    wait_bytes(k_got.at[pl.ds(1, cols - 1)], k_sem.at[0])
    for copy in side_copy:
        copy.wait_send()


def body(cols, rows, obs_values, obs_dest, obs_node, schur, local_inverse, coarse_inverse):
    size = schur.shape[-1]
    edge = size // 4
    realiz = obs_values.shape[1]
    obs = obs_values.shape[0]
    count = coarse_inverse.shape[1]
    vmem = pl.BlockSpec(memory_space=pltpu.VMEM)
    hbm = pl.BlockSpec(memory_space=pltpu.HBM)
    vector = pltpu.VMEM((realiz, size), F32)
    halved = pltpu.VMEM((2 * realiz, size), BF16)
    out = jax.ShapeDtypeStruct((realiz, size), F32)
    dma = pltpu.SemaphoreType.DMA
    found, residual = pl.pallas_call(
        functools.partial(kernel, cols, rows),
        out_shape=(out, out),
        in_specs=[hbm] * 6,
        out_specs=(vmem, vmem),
        scratch_shapes=[
            pltpu.VMEM((realiz, obs), BF16),
            pltpu.VMEM((1, obs), jnp.int32),
            pltpu.VMEM((1, obs), jnp.int32),
            pltpu.VMEM((8, count), F32),
            pltpu.VMEM((size, size), BF16),
            pltpu.VMEM((size, size), BF16),
            pltpu.VMEM((cols, rows // 2, 8, 128), BF16),
            pltpu.VMEM((cols, rows // 2, 8, 128), BF16),
            pltpu.VMEM((rows, cols, 8, 128), BF16),
            pltpu.VMEM((cols, 8, 128), F32),
            pltpu.VMEM((cols, 8, 128), F32),
            pltpu.VMEM((cols * 8, 128), F32),
            pltpu.VMEM((2, cols * 8, 128), F32),
            pltpu.VMEM((cols * 8, 3 * 8 * rows), BF16),
            halved, halved,
            vector, vector, vector, vector, vector, vector,
            pltpu.VMEM((16, size), BF16),
            pltpu.VMEM((8, realiz, edge), BF16),
            pltpu.VMEM((12, realiz, edge), BF16),
            pltpu.VMEM((8, realiz, edge), BF16),
            pltpu.VMEM((12, realiz, edge), BF16),
            pltpu.VMEM((8, 128), F32),
            pltpu.VMEM((2, rows, 8, 128), F32),
            pltpu.VMEM((cols, 8, 128), F32),
            pltpu.VMEM((2, cols, 8, 128), F32),
            pltpu.VMEM((3, realiz, 128), F32), vector,
            dma((4,)), dma((2,)), dma((4,)), dma((2,)), dma((2, 2)),
            dma((2, 12)), dma((2, 12)), dma((2,)), dma((2,)), dma((2,)),
        ],
        compiler_params=pltpu.CompilerParams(
            collective_id=0, has_side_effects=True, vmem_limit_bytes=48 << 20
        ),
    )(
        obs_values.T, obs_dest.reshape(1, obs), obs_node.reshape(1, obs),
        schur, local_inverse, coarse_inverse,
    )
    return found[None, None], residual[None, None]


def solution(mesh):
    placed = (
        P(("sx", "sy"), None),
        P(("sx", "sy"), None),
        P(("sx", "sy")),
        P("sx", "sy", None, None),
        P("sx", "sy", None, None),
        P(("sx", "sy"), None),
    )
    return jax.shard_map(
        functools.partial(body, mesh.shape["sx"], mesh.shape["sy"]),
        mesh=mesh,
        in_specs=placed,
        out_specs=(P("sx", "sy", None, None), P("sx", "sy", None, None)),
        check_vma=False,
    )
```

time: 142 us -> 110 us (0.77)
  Pallas kernels: 136 us -> 105 us
    pallas_call x1, Pallas kernels: 136 us -> 105 us  [body(): pl.pallas_call(functools.partial(kernel, cols, rows), out_shape=(out, out...]
    unnamed x8 -> x10, local copies, waits for them, and re-layouts: 4.71 us -> 4.45 us
where the time goes in v2:
time: 110 us
  Pallas kernels  105 us (95%)
  local copies, waits for them, and re-layouts  4.45 us (4%)
    pallas_call x1, Pallas kernels, body(): pl.pallas_call(functools.partial(kernel, cols, rows), out_shape=(out, out...  105 us
    unnamed x10, local copies, waits for them, and re-layouts  4.45 us

profile of v2, /device:TPU:1, one launch (start us, length us, event | category | flops | bytes accessed | tf_op | source)
XLA Modules:
  0.0 109.7 jit_solution(13263909180452846316)
XLA Ops:
  0.6 0.0 copy-start
  0.6 0.7 copy-done
  1.4 0.0 copy-start.1
  1.4 0.8 copy-done.1
  2.1 0.0 copy-start.2
  2.2 0.7 copy-done.2
  2.8 0.0 copy-start.3
  2.8 0.7 copy-done.3
  3.5 104.6 %shard_map.77 = (f32[64,2048]{1,0:T(8,128)S(1)}, f32[64,2048]{1,0:T(8,128)S(1)}) custom-call(bf16[64,256]{1,0:T(8,128)(2,1)S(1)} %bitcast.7, s32[1,256]{1,0:T(1,128)S(1)} %bitcast.8, s32[1,256]{1,0:T(1,128)S(1)} %bitcast.9, bf16[1,1,2048,2048]{3,2,1,0:T(8,128)(2,1)} %schur_hbm.1, bf16[1,1,2048,2048]{3,2,1,0:T(8,128)(2,1)} %inverse_hbm.1, f32[8,1024]{1,0:T(8,128)S(1)} %copy-done.1), custom_call_target="tpu_custom_call" | custom-call | tf_op jit(solution)/shard_map/pallas_call | solution.py:481
  108.1 0.8 copy.10
  108.9 0.8 copy.11
Async XLA Ops:
  0.6 0.8 copy-start
  1.4 0.8 copy-start.1
  2.1 0.7 copy-start.2
  2.8 0.7 copy-start.3

commit v3 on v2

--- a/solution.py
+++ b/solution.py
@@ -33,7 +33,7 @@
     x_ref, r_ref,
     values_ref, dest_ref, node_ref, coarse_ref, schur, inverse,
     obs_send, obs_mid, obs_got, k_send, k_got, k_row, k_side, k_cat,
-    zb_ref, yb_ref, d_ref, s_ref, t_ref, z_ref, y_ref, h_ref, sb_ref,
+    zb_ref, yb_ref, d_ref, s_ref, t_ref, z_ref, y_ref, h_ref, acc_ref, acc_g, sb_ref,
     lin_send, lin_got, sch_send, sch_got,
     pay1, got1, pay2, got2, state, late_ref,
     in_sem, mat_sem, obs_sem, k_sem, side_sem, lin_sem, sch_sem, one_sem, two_sem, out_sem,
@@ -279,12 +279,30 @@
         yb_ref[0:realiz, span[e]] = high
         yb_ref[realiz:, span[e]] = low
 
+    half = 2 * edge
+
+    def begin_product(operand, matrix):
+        for e in range(4):
+            acc_ref[:, span[e]] = jnp.dot(
+                operand[:, half:], matrix[half:, span[e]], preferred_element_type=F32
+            )
+
+    def begin_g():
+        acc_g[...] = lax.dot_general(
+            sb_ref[:, half:], zb_ref[:, half:], NT, preferred_element_type=F32
+        )
+
+    def end_product(operand, matrix, e):
+        return acc_ref[:, span[e]] + jnp.dot(
+            operand[:, :half], matrix[:half, span[e]], preferred_element_type=F32
+        )
+
     def apply_inverse(parity):
+        pass_payload(parity)
         for e in (2, 3):
             take_high(e)
             y_ref[:, span[e]] = finish_image(e, parity)
             put_y(e)
-        pass_payload(parity)
         for e in (0, 1):
             take_high(e)
             put_y(e)
@@ -311,7 +329,6 @@
         return mask[e] * lin_got[e].astype(F32)
 
     def take_low(e, alpha, once, parity):
-        lin_copy(4 + e, parity).wait_send()
         lin_copy(4 + opposite[e], parity).wait_recv()
         low = mask[e] * lin_got[4 + 4 * parity + e].astype(F32)
         t_ref[:, span[e]] = t_ref[:, span[e]] + once * low
@@ -371,6 +388,9 @@
     total = take_payload(1)
     for e in (2, 3, 0, 1):
         put_z(e, h_ref[:, span[e]] + coarse_part(e, total) + take_lin(e))
+        if e == 3:
+            begin_product(zb_ref, schur)
+            begin_g()
     state[2] = -jnp.ones_like(state[2])
 
     def apply_schur(parity):
@@ -378,7 +398,7 @@
         sum_zy = jnp.zeros((realiz, 128), F32)
         sum_zs = jnp.zeros((realiz, 128), F32)
         for e in range(4):
-            made = jnp.dot(zb_ref[...], schur[:, span[e]], preferred_element_type=F32)
+            made = end_product(zb_ref, schur, e)
             y = made[0:realiz] + made[realiz:]
             send_partial(e, y)
             z = z_ref[:, span[e]]
@@ -389,7 +409,9 @@
                 sum_rz += rz[:, tile]
                 sum_zy += zy[:, tile]
                 sum_zs += zs[:, tile]
-        made = lax.dot_general(sb_ref[...], zb_ref[...], NT, preferred_element_type=F32)
+        made = acc_g[...] + lax.dot_general(
+            sb_ref[:, :half], zb_ref[:, :half], NT, preferred_element_type=F32
+        )
         made = made[0:8] + made[8:16]
         pay1[:, 0:realiz] = made[:, 0:realiz] + made[:, realiz:]
         lane = lax.broadcasted_iota(jnp.int32, (realiz, 128), 1)
@@ -427,8 +449,10 @@
         parity = lax.rem(k, 2)
         apply_schur(parity)
         for e in range(4):
+            lin_copy(4 + e, 1 - parity).wait_send()
+        apply_inverse(parity)
+        for e in range(4):
             take_low(e, state[2, :, 0:1], jnp.where(k > 0, 1.0, 0.0).astype(F32), 1 - parity)
-        apply_inverse(parity)
         for e in (0, 1):
             y_ref[:, span[e]] = finish_image(e, parity)
         total = take_payload(parity)
@@ -443,6 +467,9 @@
             came = take_lin(e)
             t_ref[:, span[e]] = t_ref[:, span[e]] + came
             put_z(e, z_ref[:, span[e]] - alpha * came)
+            if e == 3:
+                begin_product(zb_ref, schur)
+                begin_g()
         return carry
 
     lax.fori_loop(0, ITERS - 1, step, 0)
@@ -500,6 +527,8 @@
             pltpu.VMEM((cols * 8, 3 * 8 * rows), BF16),
             halved, halved,
             vector, vector, vector, vector, vector, vector,
+            pltpu.VMEM((2 * realiz, size), F32),
+            pltpu.VMEM((16, 2 * realiz), F32),
             pltpu.VMEM((16, size), BF16),
             pltpu.VMEM((8, realiz, edge), BF16),
             pltpu.VMEM((12, realiz, edge), BF16),

time: 110 us -> 107 us (0.973)
  Pallas kernels: 105 us -> 102 us
    pallas_call x1, Pallas kernels: 105 us -> 102 us  [body(): pl.pallas_call(functools.partial(kernel, cols, rows), out_shape=(out, out...]
where the time goes in v3:
time: 107 us
  Pallas kernels  102 us (95%)
  local copies, waits for them, and re-layouts  4.45 us (4%)
    pallas_call x1, Pallas kernels, body(): pl.pallas_call(functools.partial(kernel, cols, rows), out_shape=(out, out...  102 us
    unnamed x10, local copies, waits for them, and re-layouts  4.45 us

profile of v3, /device:TPU:1, one launch (start us, length us, event | category | flops | bytes accessed | tf_op | source)
XLA Modules:
  0.0 106.6 jit_solution(268464022312328025)
XLA Ops:
  0.6 0.0 copy-start
  0.6 0.7 copy-done
  1.4 0.0 copy-start.1
  1.4 0.8 copy-done.1
  2.1 0.0 copy-start.2
  2.2 0.7 copy-done.2
  2.8 0.0 copy-start.3
  2.8 0.7 copy-done.3
  3.5 101.5 %shard_map.77 = (f32[64,2048]{1,0:T(8,128)S(1)}, f32[64,2048]{1,0:T(8,128)S(1)}) custom-call(bf16[64,256]{1,0:T(8,128)(2,1)S(1)} %bitcast.7, s32[1,256]{1,0:T(1,128)S(1)} %bitcast.8, s32[1,256]{1,0:T(1,128)S(1)} %bitcast.9, bf16[1,1,2048,2048]{3,2,1,0:T(8,128)(2,1)} %schur_hbm.1, bf16[1,1,2048,2048]{3,2,1,0:T(8,128)(2,1)} %inverse_hbm.1, f32[8,1024]{1,0:T(8,128)S(1)} %copy-done.1), custom_call_target="tpu_custom_call" | custom-call | tf_op jit(solution)/shard_map/pallas_call | solution.py:508
  105.0 0.8 copy.10
  105.8 0.8 copy.11
Async XLA Ops:
  0.6 0.8 copy-start
  1.4 0.8 copy-start.1
  2.1 0.7 copy-start.2
  2.8 0.7 copy-start.3

commit v4 on v3

--- a/solution.py
+++ b/solution.py
@@ -543,7 +543,7 @@
             dma((2, 12)), dma((2, 12)), dma((2,)), dma((2,)), dma((2,)),
         ],
         compiler_params=pltpu.CompilerParams(
-            collective_id=0, has_side_effects=True, vmem_limit_bytes=48 << 20
+            collective_id=0, has_side_effects=True, vmem_limit_bytes=60 << 20
         ),
     )(
         obs_values.T, obs_dest.reshape(1, obs), obs_node.reshape(1, obs),

time: 107 us -> 107 us (level)
    unnamed x10 -> x2, local copies, waits for them, and re-layouts: 4.45 us -> 3.74 us
where the time goes in v4:
time: 107 us
  Pallas kernels  102 us (95%)
  local copies, waits for them, and re-layouts  3.74 us (3%)
    pallas_call x1, Pallas kernels, body(): pl.pallas_call(functools.partial(kernel, cols, rows), out_shape=(out, out...  102 us
    unnamed x2, local copies, waits for them, and re-layouts  3.74 us

profile of v4, /device:TPU:1, one launch (start us, length us, event | category | flops | bytes accessed | tf_op | source)
XLA Modules:
  0.0 106.7 jit_solution(631864652172723804)
XLA Ops:
  0.6 102.3 %shard_map.77 = (f32[64,2048]{1,0:T(8,128)}, f32[64,2048]{1,0:T(8,128)}) custom-call(bf16[64,256]{1,0:T(8,128)(2,1)} %bitcast.7, s32[1,256]{1,0:T(1,128)} %bitcast.8, s32[1,256]{1,0:T(1,128)} %bitcast.9, bf16[1,1,2048,2048]{3,2,1,0:T(8,128)(2,1)} %schur_hbm.1, bf16[1,1,2048,2048]{3,2,1,0:T(8,128)(2,1)} %inverse_hbm.1, f32[8,1024]{1,0:T(8,128)} %coarse_hbm.1), custom_call_target="tpu_custom_call" | custom-call | tf_op jit(solution)/shard_map/pallas_call | solution.py:508
  103.0 1.9 %copy.10 = f32[1,1,64,2048]{3,2,1,0:T(8,128)} copy(f32[1,1,64,2048]{3,2,1,0:T(8,128)} %bitcast.6) | data formatting | bytes 1048576
  104.8 1.9 %copy.11 = f32[1,1,64,2048]{3,2,1,0:T(8,128)} copy(f32[1,1,64,2048]{3,2,1,0:T(8,128)} %bitcast.5) | data formatting | bytes 1048576
